TPU v7x, 256 devices: a whole 4x4x8 slice. The times are simulated.
256 devices in a mesh: leaf: 64 (over z, x, core), sub: 4 (over y).
Axes of the slice: x: 4, y: 4, z: 8, core: 2. Of those that a mesh axis runs over, the one named last changes fastest.
Arguments:
- coords: bfloat16 [32768, 3, 128], P('leaf'), may hold values from 0 to 4
- charges: bfloat16 [32768, 8, 128], P(('leaf', 'sub')), may hold values from -6 to 6
- counts: int32 [32768], P('leaf'), may hold values from 32 to 128, as said below
- morton: int32 [32768], P('leaf'), may hold values from 0 to 511, as said below
- near_list: int32 [32768, 27], P(('leaf', 'sub')), may hold values from -1 to 32767, as said below
- basis: bfloat16 [32768, 64, 128], P(('leaf', 'sub')), may hold values from -0.5 to 0.5
- transfer1: bfloat16 [32768, 64, 64], P(('leaf', 'sub')), may hold values from -0.75 to 0.75
- far2_list: int32 [4096, 16], P(('leaf', 'sub')), may hold values from -1 to 4095, as said below
- coupling2: bfloat16 [4096, 16, 64, 64], P(('leaf', 'sub')), may hold values from -0.0625 to 0.0625
- transfer2: bfloat16 [4096, 64, 64], P('leaf'), may hold values from -0.75 to 0.75
- far3_list: int32 [64, 8], P('leaf'), may hold values from -1 to 63, as said below
- coupling3: bfloat16 [64, 8, 64, 64], P('leaf'), may hold values from -0.01171875 to 0.01171875
Outputs:
- potential: float32 [32768, 8, 128], P(('leaf', 'sub'))
Inputs may be any that keep to these rules, and one draw needn't show every extreme that they name: `counts`: each leaf's number of live points; leaves do not all have the same number. `morton`: within every block of 512 consecutive entries, a permutation of 0 to 511. `near_list`: row t starts with t itself; its other live entries are leaves other than t in the leaf group of t or in the group just before or after it; live entries come first and -1 fills the rest, with at least 13 live entries a row; entries may repeat. `far2_list`: row b names boxes other than b in the leaf group of b or in the group just before or after it; live entries come first and -1 fills the rest, with at least 8 live entries a row; entries may repeat. `far3_list`: row q names group boxes other than q; live entries come first and -1 fills the rest, with at least 4 live entries a row; entries may repeat.
All inputs are finite; a program needn't handle non-finite values.
Results may differ from a plain program's by a relative error of at most 0.011.
Values may be sent and summed in bfloat16 or wider, within the bound.
No kernel may reach another device: no remote copies, remote signals or barrier semaphores. Data moves between devices by JAX's collectives and lax.ppermute only.
A program may use at most 64 MiB of HBM per device.

v0:
```python
import jax
import jax.numpy as jnp
from jax import lax
from jax.sharding import PartitionSpec as P

kernel_scale = 0.07957747154594767
delta_squared = 0.0025


def with_halo(cells, sides, width):
    for axis, dim in sides:
        count = lax.axis_size(axis)
        ends = count - 1
        head = lax.slice_in_dim(cells, 0, width, axis=dim)
        tail = lax.slice_in_dim(cells, cells.shape[dim] - width, cells.shape[dim], axis=dim)
        cells = jnp.concatenate(
            [
                lax.ppermute(tail, axis, [(i, (i + 1) % count) for i in range(ends)]),
                cells,
                lax.ppermute(head, axis, [((i + 1) % count, i) for i in range(ends)]),
            ],
            axis=dim,
        )
    return cells


def kernel_tile(targets, sources):
    squared = jnp.zeros((targets.shape[0], targets.shape[2], sources.shape[2]), jnp.float32)
    for component in range(3):
        offset = targets[:, component, :, None] - sources[:, component, None, :]
        squared = squared + offset * offset
    return (kernel_scale / jnp.sqrt(squared + delta_squared)).astype(jnp.bfloat16)


def far_field(moments, lists, couplings, offset):
    valid = lists >= 0
    local = jnp.clip(lists - offset, 0, moments.shape[0] - 1)
    source = jnp.where(valid[..., None, None], moments[local], jnp.zeros((), moments.dtype))
    return jnp.einsum("bkrc,bkcp->brp", source, couplings, preferred_element_type=jnp.float32)


def on_device(
    coords,
    charges,
    counts,
    morton,
    near_list,
    basis,
    transfer1,
    far2_list,
    coupling2,
    transfer2,
    far3_list,
    coupling3,
):
    lane = lax.axis_index("sub")
    group = lax.axis_index("leaf")
    leaf_dev = charges.shape[0]
    rhs_count = charges.shape[1]
    points = charges.shape[2]
    rank_size = basis.shape[1]
    group_size = coords.shape[0]
    clusters = far2_list.shape[0]
    group_boxes = transfer2.shape[0]
    start = lane * leaf_dev
    arrived = lax.all_gather(charges, "sub", axis=0, tiled=True)
    inverse = (
        jnp.zeros((group_size,), jnp.int32).at[morton].set(jnp.arange(group_size, dtype=jnp.int32))
    )
    ordered = arrived[inverse]
    live = jnp.arange(points, dtype=jnp.int32)[None, :] < counts[:, None]
    masked = jnp.where(live[:, None, :], ordered, jnp.zeros((), ordered.dtype))
    packed = jnp.concatenate([coords, masked], axis=1)
    nearby = with_halo(packed, (("leaf", 0),), group_size)
    own_charges = lax.dynamic_slice_in_dim(masked, start, leaf_dev, 0)
    own_live = lax.dynamic_slice_in_dim(live, start, leaf_dev, 0)
    targets = lax.dynamic_slice_in_dim(coords, start, leaf_dev, 0).astype(jnp.float32)
    transfer_boxed = transfer1.reshape(clusters, 8, rank_size, rank_size)
    leaf_moments = jnp.einsum(
        "trp,tkp->trk", own_charges, basis, preferred_element_type=jnp.float32
    ).astype(jnp.bfloat16)
    box_moments = jnp.einsum(
        "bnrc,bncp->brp",
        leaf_moments.reshape(clusters, 8, rhs_count, rank_size),
        transfer_boxed,
        preferred_element_type=jnp.float32,
    ).astype(jnp.bfloat16)
    group_moments = lax.all_gather(box_moments, "sub", axis=0, tiled=True)
    top_moment = jnp.einsum(
        "brc,bcp->rp", group_moments, transfer2, preferred_element_type=jnp.float32
    ).astype(jnp.bfloat16)
    all_top = lax.all_gather(top_moment[None], "leaf", axis=0, tiled=True)
    near_boxes = with_halo(group_moments, (("leaf", 0),), group_boxes)
    top_field = far_field(all_top, far3_list, coupling3, 0).astype(jnp.bfloat16)
    box_far = far_field(near_boxes, far2_list, coupling2, (group - 1) * group_boxes)
    own_transfer = lax.dynamic_slice_in_dim(transfer2, lane * clusters, clusters, 0)
    box_local = (
        box_far
        + jnp.einsum("rp,bcp->brc", top_field[0], own_transfer, preferred_element_type=jnp.float32)
    ).astype(jnp.bfloat16)
    leaf_local = jnp.einsum(
        "brp,bncp->bnrc", box_local, transfer_boxed, preferred_element_type=jnp.float32
    ).astype(jnp.bfloat16)
    leaf_local = leaf_local.reshape(leaf_dev, rhs_count, rank_size)
    far_part = jnp.einsum("trk,tkp->trp", leaf_local, basis, preferred_element_type=jnp.float32)
    base = (group - 1) * group_size

    def slot_step(total, column):
        valid = column >= 0
        index = jnp.clip(column - base, 0, 3 * group_size - 1)
        rows = nearby[index]
        tile = kernel_tile(targets, rows[:, :3].astype(jnp.float32))
        source = jnp.where(valid[:, None, None], rows[:, 3:], jnp.zeros((), rows.dtype))
        return (
            total + jnp.einsum("tij,trj->tri", tile, source, preferred_element_type=jnp.float32),
            None,
        )

    near_part, unused = lax.scan(
        slot_step, jnp.zeros((leaf_dev, rhs_count, points), jnp.float32), near_list.T
    )
    return jnp.where(own_live[:, None, :], near_part + far_part, jnp.zeros((), jnp.float32))


def solution(mesh):
    return jax.shard_map(
        on_device,
        mesh=mesh,
        in_specs=(
            P("leaf", None, None),
            P(("leaf", "sub"), None, None),
            P("leaf"),
            P("leaf"),
            P(("leaf", "sub"), None),
            P(("leaf", "sub"), None, None),
            P(("leaf", "sub"), None, None),
            P(("leaf", "sub"), None),
            P(("leaf", "sub"), None, None, None),
            P("leaf", None, None),
            P("leaf", None),
            P("leaf", None, None, None),
        ),
        out_specs=P(("leaf", "sub"), None, None),
        check_vma=False,
    )
```

profile of v0, /device:TPU:1, one launch (start us, length us, event | category | flops | bytes accessed | tf_op | source)
XLA Modules:
  0.0 683.8 jit_solution(16244068060757462938)
XLA Ops:
  19.3 19.4 %all-gather.3.cloned.1.call-done = bf16[512,8,128]{2,1,0:T(8,128)(2,1)} async-done(((bf16[128,8,128]{2,1,0:T(8,128)(2,1)}), bf16[512,8,128]{2,1,0:T(8,128)(2,1)}) %all-gather.3.cloned.1.call-update) | async-done | bytes 1048592 | tf_op jit(solution)/shard_map/all_gather | solution.py:66
  72.1 72.7 %all-gather = bf16[512,64]{1,0:T(8,128)(2,1)} all-gather(bf16[8,64]{1,0:T(8,128)(2,1)S(1)} %fusion.12), channel_id=2, replica_groups=mesh['leaf'=64,'sub'=4] {'leaf'}, dimensions={0}, use_global_device_ids=true | all-gather | bytes 66560 | tf_op jit(solution)/shard_map/all_gather | solution.py:92
  167.0 25.8 %pad_maximum_fusion = bf16[1536,11,128]{2,1,0:T(8,128)(2,1)} fusion(bf16[512,11,128]{2,1,0:T(8,128)(2,1)S(1)} %copy.22, bf16[512,8,128]{2,1,0:T(8,128)(2,1)S(1)} %broadcast_select_fusion, bf16[512,3,128]{2,1,0:T(4,128)(2,1)S(1)} %copy-done.3, bf16[512,11,128]{2,1,0:T(8,128)(2,1)S(1)} %copy.21), kind=kLoop, calls=%fused_computation.23 | loop fusion | flops 17301504 | bytes 8650752 | tf_op jit(solution)/shard_map/concatenate | solution.py:16
  192.7 482.2 %while.11 = (s32[]{:T(128)}, f32[128,8,128]{2,1,0:T(8,128)}, s32[27,128]{1,0:T(8,128)}, s32[]{:T(128)}, bf16[1536,11,128]{2,1,0:T(8,128)(2,1)}, /*index=5*/f32[128,3,128]{2,0,1:T(8,128)S(1)}, s32[]{:T(128)}, s32[]{:T(128)}) while((s32[]{:T(128)}, f32[128,8,128]{2,1,0:T(8,128)}, s32[27,128]{1,0:T(8,128)}, s32[]{:T(128)}, ...), condition=%wide.region_2.3_spmd.clone, body=%wide.region_1.2_spmd.clone.sunk | while | flops 57067264 | bytes 3513195 | solution.py:119
  216.9 11.6 %fusion.50 = f32[128,8,128]{2,1,0:T(8,128)} fusion(f32[128,128]{1,0:T(8,128)S(1)} %bitcast.93, f32[128,128]{1,0:T(8,128)} %get-tuple-element.121, f32[128,128]{1,0:T(8,128)S(1)} %bitcast.94, f32[128,128]{1,0:T(8,128)} %get-tuple-element.123, f32[128,128]{1,0:T(8,128)S(1)} %bitcast.92, f32[128,128]{1,0:T(8,128)} %get-tuple-element.125, ...), kind=kOutput, calls=%fused_computation.7.clone.1 | convolution fusion | flops 57016320 | bytes 1704065 | tf_op jit(solution)/shard_map/while/body/eval_jaxpr/tij,trj->tri/dot_general | solution.py:115
  234.7 11.6 %fusion.50 = f32[128,8,128]{2,1,0:T(8,128)} fusion(f32[128,128]{1,0:T(8,128)S(1)} %bitcast.93, f32[128,128]{1,0:T(8,128)} %get-tuple-element.121, f32[128,128]{1,0:T(8,128)S(1)} %bitcast.94, f32[128,128]{1,0:T(8,128)} %get-tuple-element.123, f32[128,128]{1,0:T(8,128)S(1)} %bitcast.92, f32[128,128]{1,0:T(8,128)} %get-tuple-element.125, ...), kind=kOutput, calls=%fused_computation.7.clone.1 | convolution fusion | flops 57016320 | bytes 1704065 | tf_op jit(solution)/shard_map/while/body/eval_jaxpr/tij,trj->tri/dot_general | solution.py:115
  252.6 11.6 %fusion.50 = f32[128,8,128]{2,1,0:T(8,128)} fusion(f32[128,128]{1,0:T(8,128)S(1)} %bitcast.93, f32[128,128]{1,0:T(8,128)} %get-tuple-element.121, f32[128,128]{1,0:T(8,128)S(1)} %bitcast.94, f32[128,128]{1,0:T(8,128)} %get-tuple-element.123, f32[128,128]{1,0:T(8,128)S(1)} %bitcast.92, f32[128,128]{1,0:T(8,128)} %get-tuple-element.125, ...), kind=kOutput, calls=%fused_computation.7.clone.1 | convolution fusion | flops 57016320 | bytes 1704065 | tf_op jit(solution)/shard_map/while/body/eval_jaxpr/tij,trj->tri/dot_general | solution.py:115
  270.5 11.6 %fusion.50 = f32[128,8,128]{2,1,0:T(8,128)} fusion(f32[128,128]{1,0:T(8,128)S(1)} %bitcast.93, f32[128,128]{1,0:T(8,128)} %get-tuple-element.121, f32[128,128]{1,0:T(8,128)S(1)} %bitcast.94, f32[128,128]{1,0:T(8,128)} %get-tuple-element.123, f32[128,128]{1,0:T(8,128)S(1)} %bitcast.92, f32[128,128]{1,0:T(8,128)} %get-tuple-element.125, ...), kind=kOutput, calls=%fused_computation.7.clone.1 | convolution fusion | flops 57016320 | bytes 1704065 | tf_op jit(solution)/shard_map/while/body/eval_jaxpr/tij,trj->tri/dot_general | solution.py:115
  288.3 11.6 %fusion.50 = f32[128,8,128]{2,1,0:T(8,128)} fusion(f32[128,128]{1,0:T(8,128)S(1)} %bitcast.93, f32[128,128]{1,0:T(8,128)} %get-tuple-element.121, f32[128,128]{1,0:T(8,128)S(1)} %bitcast.94, f32[128,128]{1,0:T(8,128)} %get-tuple-element.123, f32[128,128]{1,0:T(8,128)S(1)} %bitcast.92, f32[128,128]{1,0:T(8,128)} %get-tuple-element.125, ...), kind=kOutput, calls=%fused_computation.7.clone.1 | convolution fusion | flops 57016320 | bytes 1704065 | tf_op jit(solution)/shard_map/while/body/eval_jaxpr/tij,trj->tri/dot_general | solution.py:115
  306.2 11.6 %fusion.50 = f32[128,8,128]{2,1,0:T(8,128)} fusion(f32[128,128]{1,0:T(8,128)S(1)} %bitcast.93, f32[128,128]{1,0:T(8,128)} %get-tuple-element.121, f32[128,128]{1,0:T(8,128)S(1)} %bitcast.94, f32[128,128]{1,0:T(8,128)} %get-tuple-element.123, f32[128,128]{1,0:T(8,128)S(1)} %bitcast.92, f32[128,128]{1,0:T(8,128)} %get-tuple-element.125, ...), kind=kOutput, calls=%fused_computation.7.clone.1 | convolution fusion | flops 57016320 | bytes 1704065 | tf_op jit(solution)/shard_map/while/body/eval_jaxpr/tij,trj->tri/dot_general | solution.py:115
  324.1 11.6 %fusion.50 = f32[128,8,128]{2,1,0:T(8,128)} fusion(f32[128,128]{1,0:T(8,128)S(1)} %bitcast.93, f32[128,128]{1,0:T(8,128)} %get-tuple-element.121, f32[128,128]{1,0:T(8,128)S(1)} %bitcast.94, f32[128,128]{1,0:T(8,128)} %get-tuple-element.123, f32[128,128]{1,0:T(8,128)S(1)} %bitcast.92, f32[128,128]{1,0:T(8,128)} %get-tuple-element.125, ...), kind=kOutput, calls=%fused_computation.7.clone.1 | convolution fusion | flops 57016320 | bytes 1704065 | tf_op jit(solution)/shard_map/while/body/eval_jaxpr/tij,trj->tri/dot_general | solution.py:115
  341.9 11.6 %fusion.50 = f32[128,8,128]{2,1,0:T(8,128)} fusion(f32[128,128]{1,0:T(8,128)S(1)} %bitcast.93, f32[128,128]{1,0:T(8,128)} %get-tuple-element.121, f32[128,128]{1,0:T(8,128)S(1)} %bitcast.94, f32[128,128]{1,0:T(8,128)} %get-tuple-element.123, f32[128,128]{1,0:T(8,128)S(1)} %bitcast.92, f32[128,128]{1,0:T(8,128)} %get-tuple-element.125, ...), kind=kOutput, calls=%fused_computation.7.clone.1 | convolution fusion | flops 57016320 | bytes 1704065 | tf_op jit(solution)/shard_map/while/body/eval_jaxpr/tij,trj->tri/dot_general | solution.py:115
  359.8 11.6 %fusion.50 = f32[128,8,128]{2,1,0:T(8,128)} fusion(f32[128,128]{1,0:T(8,128)S(1)} %bitcast.93, f32[128,128]{1,0:T(8,128)} %get-tuple-element.121, f32[128,128]{1,0:T(8,128)S(1)} %bitcast.94, f32[128,128]{1,0:T(8,128)} %get-tuple-element.123, f32[128,128]{1,0:T(8,128)S(1)} %bitcast.92, f32[128,128]{1,0:T(8,128)} %get-tuple-element.125, ...), kind=kOutput, calls=%fused_computation.7.clone.1 | convolution fusion | flops 57016320 | bytes 1704065 | tf_op jit(solution)/shard_map/while/body/eval_jaxpr/tij,trj->tri/dot_general | solution.py:115
  377.6 11.6 %fusion.50 = f32[128,8,128]{2,1,0:T(8,128)} fusion(f32[128,128]{1,0:T(8,128)S(1)} %bitcast.93, f32[128,128]{1,0:T(8,128)} %get-tuple-element.121, f32[128,128]{1,0:T(8,128)S(1)} %bitcast.94, f32[128,128]{1,0:T(8,128)} %get-tuple-element.123, f32[128,128]{1,0:T(8,128)S(1)} %bitcast.92, f32[128,128]{1,0:T(8,128)} %get-tuple-element.125, ...), kind=kOutput, calls=%fused_computation.7.clone.1 | convolution fusion | flops 57016320 | bytes 1704065 | tf_op jit(solution)/shard_map/while/body/eval_jaxpr/tij,trj->tri/dot_general | solution.py:115
  395.5 11.6 %fusion.50 = f32[128,8,128]{2,1,0:T(8,128)} fusion(f32[128,128]{1,0:T(8,128)S(1)} %bitcast.93, f32[128,128]{1,0:T(8,128)} %get-tuple-element.121, f32[128,128]{1,0:T(8,128)S(1)} %bitcast.94, f32[128,128]{1,0:T(8,128)} %get-tuple-element.123, f32[128,128]{1,0:T(8,128)S(1)} %bitcast.92, f32[128,128]{1,0:T(8,128)} %get-tuple-element.125, ...), kind=kOutput, calls=%fused_computation.7.clone.1 | convolution fusion | flops 57016320 | bytes 1704065 | tf_op jit(solution)/shard_map/while/body/eval_jaxpr/tij,trj->tri/dot_general | solution.py:115
  413.4 11.6 %fusion.50 = f32[128,8,128]{2,1,0:T(8,128)} fusion(f32[128,128]{1,0:T(8,128)S(1)} %bitcast.93, f32[128,128]{1,0:T(8,128)} %get-tuple-element.121, f32[128,128]{1,0:T(8,128)S(1)} %bitcast.94, f32[128,128]{1,0:T(8,128)} %get-tuple-element.123, f32[128,128]{1,0:T(8,128)S(1)} %bitcast.92, f32[128,128]{1,0:T(8,128)} %get-tuple-element.125, ...), kind=kOutput, calls=%fused_computation.7.clone.1 | convolution fusion | flops 57016320 | bytes 1704065 | tf_op jit(solution)/shard_map/while/body/eval_jaxpr/tij,trj->tri/dot_general | solution.py:115
  431.2 11.6 %fusion.50 = f32[128,8,128]{2,1,0:T(8,128)} fusion(f32[128,128]{1,0:T(8,128)S(1)} %bitcast.93, f32[128,128]{1,0:T(8,128)} %get-tuple-element.121, f32[128,128]{1,0:T(8,128)S(1)} %bitcast.94, f32[128,128]{1,0:T(8,128)} %get-tuple-element.123, f32[128,128]{1,0:T(8,128)S(1)} %bitcast.92, f32[128,128]{1,0:T(8,128)} %get-tuple-element.125, ...), kind=kOutput, calls=%fused_computation.7.clone.1 | convolution fusion | flops 57016320 | bytes 1704065 | tf_op jit(solution)/shard_map/while/body/eval_jaxpr/tij,trj->tri/dot_general | solution.py:115
  467.0 11.6 %fusion.50 = f32[128,8,128]{2,1,0:T(8,128)} fusion(f32[128,128]{1,0:T(8,128)S(1)} %bitcast.93, f32[128,128]{1,0:T(8,128)} %get-tuple-element.121, f32[128,128]{1,0:T(8,128)S(1)} %bitcast.94, f32[128,128]{1,0:T(8,128)} %get-tuple-element.123, f32[128,128]{1,0:T(8,128)S(1)} %bitcast.92, f32[128,128]{1,0:T(8,128)} %get-tuple-element.125, ...), kind=kOutput, calls=%fused_computation.7.clone.1 | convolution fusion | flops 57016320 | bytes 1704065 | tf_op jit(solution)/shard_map/while/body/eval_jaxpr/tij,trj->tri/dot_general | solution.py:115
  484.8 11.6 %fusion.50 = f32[128,8,128]{2,1,0:T(8,128)} fusion(f32[128,128]{1,0:T(8,128)S(1)} %bitcast.93, f32[128,128]{1,0:T(8,128)} %get-tuple-element.121, f32[128,128]{1,0:T(8,128)S(1)} %bitcast.94, f32[128,128]{1,0:T(8,128)} %get-tuple-element.123, f32[128,128]{1,0:T(8,128)S(1)} %bitcast.92, f32[128,128]{1,0:T(8,128)} %get-tuple-element.125, ...), kind=kOutput, calls=%fused_computation.7.clone.1 | convolution fusion | flops 57016320 | bytes 1704065 | tf_op jit(solution)/shard_map/while/body/eval_jaxpr/tij,trj->tri/dot_general | solution.py:115
  502.7 11.6 %fusion.50 = f32[128,8,128]{2,1,0:T(8,128)} fusion(f32[128,128]{1,0:T(8,128)S(1)} %bitcast.93, f32[128,128]{1,0:T(8,128)} %get-tuple-element.121, f32[128,128]{1,0:T(8,128)S(1)} %bitcast.94, f32[128,128]{1,0:T(8,128)} %get-tuple-element.123, f32[128,128]{1,0:T(8,128)S(1)} %bitcast.92, f32[128,128]{1,0:T(8,128)} %get-tuple-element.125, ...), kind=kOutput, calls=%fused_computation.7.clone.1 | convolution fusion | flops 57016320 | bytes 1704065 | tf_op jit(solution)/shard_map/while/body/eval_jaxpr/tij,trj->tri/dot_general | solution.py:115
  520.5 11.6 %fusion.50 = f32[128,8,128]{2,1,0:T(8,128)} fusion(f32[128,128]{1,0:T(8,128)S(1)} %bitcast.93, f32[128,128]{1,0:T(8,128)} %get-tuple-element.121, f32[128,128]{1,0:T(8,128)S(1)} %bitcast.94, f32[128,128]{1,0:T(8,128)} %get-tuple-element.123, f32[128,128]{1,0:T(8,128)S(1)} %bitcast.92, f32[128,128]{1,0:T(8,128)} %get-tuple-element.125, ...), kind=kOutput, calls=%fused_computation.7.clone.1 | convolution fusion | flops 57016320 | bytes 1704065 | tf_op jit(solution)/shard_map/while/body/eval_jaxpr/tij,trj->tri/dot_general | solution.py:115
  538.4 11.6 %fusion.50 = f32[128,8,128]{2,1,0:T(8,128)} fusion(f32[128,128]{1,0:T(8,128)S(1)} %bitcast.93, f32[128,128]{1,0:T(8,128)} %get-tuple-element.121, f32[128,128]{1,0:T(8,128)S(1)} %bitcast.94, f32[128,128]{1,0:T(8,128)} %get-tuple-element.123, f32[128,128]{1,0:T(8,128)S(1)} %bitcast.92, f32[128,128]{1,0:T(8,128)} %get-tuple-element.125, ...), kind=kOutput, calls=%fused_computation.7.clone.1 | convolution fusion | flops 57016320 | bytes 1704065 | tf_op jit(solution)/shard_map/while/body/eval_jaxpr/tij,trj->tri/dot_general | solution.py:115
  556.3 11.6 %fusion.50 = f32[128,8,128]{2,1,0:T(8,128)} fusion(f32[128,128]{1,0:T(8,128)S(1)} %bitcast.93, f32[128,128]{1,0:T(8,128)} %get-tuple-element.121, f32[128,128]{1,0:T(8,128)S(1)} %bitcast.94, f32[128,128]{1,0:T(8,128)} %get-tuple-element.123, f32[128,128]{1,0:T(8,128)S(1)} %bitcast.92, f32[128,128]{1,0:T(8,128)} %get-tuple-element.125, ...), kind=kOutput, calls=%fused_computation.7.clone.1 | convolution fusion | flops 57016320 | bytes 1704065 | tf_op jit(solution)/shard_map/while/body/eval_jaxpr/tij,trj->tri/dot_general | solution.py:115
  574.1 11.6 %fusion.50 = f32[128,8,128]{2,1,0:T(8,128)} fusion(f32[128,128]{1,0:T(8,128)S(1)} %bitcast.93, f32[128,128]{1,0:T(8,128)} %get-tuple-element.121, f32[128,128]{1,0:T(8,128)S(1)} %bitcast.94, f32[128,128]{1,0:T(8,128)} %get-tuple-element.123, f32[128,128]{1,0:T(8,128)S(1)} %bitcast.92, f32[128,128]{1,0:T(8,128)} %get-tuple-element.125, ...), kind=kOutput, calls=%fused_computation.7.clone.1 | convolution fusion | flops 57016320 | bytes 1704065 | tf_op jit(solution)/shard_map/while/body/eval_jaxpr/tij,trj->tri/dot_general | solution.py:115
  (260 shorter events, 320.2 us)
Async XLA Ops:
  6.5 37.1 %copy-start = (bf16[128,64,128]{2,1,0:T(8,128)(2,1)S(1)}, bf16[128,64,128]{2,1,0:T(8,128)(2,1)}, u32[]{:S(2)}) copy-start(bf16[128,64,128]{2,1,0:T(8,128)(2,1)} %param.19) | copy-start | bytes 6291460
  6.5 12.7 %copy-start.6 = (s32[16,16]{1,0:T(8,128)S(1)}, s32[16,16]{1,0:T(8,128)}, u32[]{:S(2)}) copy-start(s32[16,16]{1,0:T(8,128)} %param.21) | copy-start | bytes 3076
  6.5 11.6 %copy-start.8 = (s32[1,8]{1,0:T(1,128)S(1)}, s32[1,8]{1,0:T(1,128)}, u32[]{:S(2)}) copy-start(s32[1,8]{1,0:T(1,128)} %param.24) | copy-start | bytes 100
  6.5 11.6 %copy-start.7 = (s32[512]{0:T(512)S(1)}, s32[512]{0:T(512)}, u32[]{:S(2)}) copy-start(s32[512]{0:T(512)} %param.16) | copy-start | bytes 6148
  6.5 32.1 %all-gather.3.cloned.1.call-start = ((), (), s32[]{:S(2)}) async-start(), calls=%async_computation | async-start | bytes 1310720 | tf_op jit(solution)/shard_map/all_gather | solution.py:66
  42.0 2.9 copy-start.1
  42.0 21.9 %copy-start.2 = (bf16[512,3,128]{2,1,0:T(4,128)(2,1)S(1)}, bf16[512,3,128]{2,1,0:T(4,128)(2,1)}, u32[]{:S(2)}) copy-start(bf16[512,3,128]{2,1,0:T(4,128)(2,1)} %copy.18) | copy-start | bytes 1179652
  45.3 26.5 %copy-start.5 = (bf16[64,64,64]{2,1,0:T(8,128)(2,1)S(1)}, bf16[64,64,64]{2,1,0:T(8,128)(2,1)}, u32[]{:S(2)}) copy-start(bf16[64,64,64]{2,1,0:T(8,128)(2,1)} %param.23) | copy-start | bytes 1572868
  54.8 92.6 %collective-permute-start.2 = (bf16[64,8,64]{2,1,0:T(8,128)(2,1)S(1)}, bf16[64,8,64]{2,1,0:T(8,128)(2,1)}, u32[]{:S(2)}, u32[]{:S(2)}) collective-permute-start(bf16[64,8,64]{2,1,0:T(8,128)(2,1)S(1)} %all_gather.10), channel_id=1, source_target_pairs={{0,4},{4,8},{8,12},{12,16},{16,20},{20,24},{24,28},{28,32},{32,36}... | collective-permute-start | bytes 196616 | tf_op jit(solution)/shard_map/ppermute | solution.py:18
  62.0 85.5 %collective-permute-start.3 = (bf16[64,8,64]{2,1,0:T(8,128)(2,1)S(1)}, bf16[64,8,64]{2,1,0:T(8,128)(2,1)}, u32[]{:S(2)}, u32[]{:S(2)}) collective-permute-start(bf16[64,8,64]{2,1,0:T(8,128)(2,1)S(1)} %all_gather.10), channel_id=1, source_target_pairs={{4,0},{8,4},{12,8},{16,12},{20,16},{24,20},{28,24},{32,28},{36,32}... | collective-permute-start | bytes 196616 | tf_op jit(solution)/shard_map/ppermute | solution.py:20
  66.2 95.9 %collective-permute-start = (bf16[512,11,128]{2,0,1:T(8,128)(2,1)}, bf16[512,11,128]{2,0,1:T(8,128)(2,1)}, u32[]{:S(2)}, u32[]{:S(2)}) collective-permute-start(bf16[512,11,128]{2,0,1:T(8,128)(2,1)} %copy.19), channel_id=1, source_target_pairs={{0,4},{4,8},{8,12},{12,16},{16,20},{20,24},{24,28},{28,32},{32,36}... | collective-permute-start | bytes 4325384 | tf_op jit(solution)/shard_map/ppermute | solution.py:18
  69.9 94.7 %collective-permute-start.1 = (bf16[512,11,128]{2,0,1:T(8,128)(2,1)}, bf16[512,11,128]{2,0,1:T(8,128)(2,1)}, u32[]{:S(2)}, u32[]{:S(2)}) collective-permute-start(bf16[512,11,128]{2,0,1:T(8,128)(2,1)} %copy.19), channel_id=1, source_target_pairs={{4,0},{8,4},{12,8},{16,12},{20,16},{24,20},{28,24},{32,28},{36,32}... | collective-permute-start | bytes 4325384 | tf_op jit(solution)/shard_map/ppermute | solution.py:20
  162.1 4.8 copy-start.3
  192.7 482.2 %copy-start.4 = (f32[128,8,128]{2,1,0:T(8,128)S(1)}, f32[128,8,128]{2,1,0:T(8,128)}, u32[]{:S(2)}) copy-start(f32[128,8,128]{2,1,0:T(8,128)} %fusion.34) | copy-start | bytes 1572868
Sparse Core Ops, SparseCore 0:
  9.2 29.4 all-gather.2
where the time goes:
time: 689 us; the launch traced here: 684 us
  matrix products  325 us (47%)
  local copies, waits for them, and re-layouts  140 us (20%)
  other arithmetic  87.3 us (13%)
  blocking collectives  82.3 us (12%)
  waiting for transfers between devices  20.1 us (3%)
  starting transfers between devices  14.7 us (2%)
  between operations  13.6 us (2%)
    dot_general x27, matrix products, slot_step(): jnp.einsum('tij,trj->tri', tile, source, preferred_element_type=jnp.float32)  312 us
    gather x27, local copies, waits for them, and re-layouts, slot_step(): rows = nearby[index]  94.2 us
    all_gather x1, blocking collectives, on_device(): all_top = lax.all_gather(top_moment[None], 'leaf', axis=0, tiled=True)  72.7 us
    ge x27, other arithmetic, slot_step(): valid = column >= 0  32.9 us
    concatenate x2, other arithmetic, with_halo(): jnp.concatenate([lax.ppermute(tail, axis, [(i, (i + 1) % count) for i in...  27.6 us
    all_gather x1, waiting for transfers between devices, on_device(): arrived = lax.all_gather(charges, 'sub', axis=0, tiled=True)  19.4 us
    select_n x27, other arithmetic, slot_step(): rows = nearby[index]  19 us
    sub x27, local copies, waits for them, and re-layouts, kernel_tile(): offset = targets[:, component, :, None] - sources[:, component, None, :]  18.6 us
  transfers between devices with their start and end apart: 5, of which 1 were waited for; matrix products, arithmetic and copies ran while one was open for 5% of the time, Pallas kernels for 0%

commit v1 on v0

--- a/solution.py
+++ b/solution.py
@@ -89,7 +89,9 @@
     top_moment = jnp.einsum(
         "brc,bcp->rp", group_moments, transfer2, preferred_element_type=jnp.float32
     ).astype(jnp.bfloat16)
-    all_top = lax.all_gather(top_moment[None], "leaf", axis=0, tiled=True)
+    block = top_moment[None]
+    sent = jnp.stack([block] * lax.axis_size("leaf"))
+    all_top = jnp.concatenate(lax.all_to_all(sent, "leaf", 0, 0), axis=0)
     near_boxes = with_halo(group_moments, (("leaf", 0),), group_boxes)
     top_field = far_field(all_top, far3_list, coupling3, 0).astype(jnp.bfloat16)
     box_far = far_field(near_boxes, far2_list, coupling2, (group - 1) * group_boxes)

time: 689 us -> 636 us (0.923)
  blocking collectives: 82.3 us -> 9.42 us
  starting transfers between devices: 14.7 us -> 29.5 us
    all_gather x1 -> x0, blocking collectives: 72.7 us -> none  [on_device(): all_top = lax.all_gather(top_moment[None], 'leaf', axis=0, tiled=True)]
    all_to_all x0 -> x1, starting transfers between devices: none -> 14.9 us  [on_device(): all_top = jnp.concatenate(lax.all_to_all(sent, 'leaf', 0, 0), axis=0)]
  transfers between devices with their start and end apart: 5 -> 6, of which waited for: 1 -> 2; matrix products, arithmetic and copies ran while one was open for 5% -> 6% of each run, Pallas kernels for 0% -> 0%
where the time goes in v1:
time: 636 us; the launch traced here: 630 us
  matrix products  326 us (51%)
  local copies, waits for them, and re-layouts  141 us (22%)
  other arithmetic  90.5 us (14%)
  starting transfers between devices  29.5 us (5%)
  waiting for transfers between devices  19.2 us (3%)
  between operations  13.6 us (2%)
  blocking collectives  9.42 us (1%)
    dot_general x27, matrix products, slot_step(): jnp.einsum('tij,trj->tri', tile, source, preferred_element_type=jnp.float32)  312 us
    gather x27, local copies, waits for them, and re-layouts, slot_step(): rows = nearby[index]  94.2 us
    ge x27, other arithmetic, slot_step(): valid = column >= 0  33 us
    concatenate x2, other arithmetic, with_halo(): jnp.concatenate([lax.ppermute(tail, axis, [(i, (i + 1) % count) for i in...  27.4 us
    select_n x27, other arithmetic, slot_step(): rows = nearby[index]  19 us
    sub x27, local copies, waits for them, and re-layouts, kernel_tile(): offset = targets[:, component, :, None] - sources[:, component, None, :]  18.3 us
    all_gather x1, waiting for transfers between devices, on_device(): arrived = lax.all_gather(charges, 'sub', axis=0, tiled=True)  17.2 us
    all_to_all x1, starting transfers between devices, on_device(): all_top = jnp.concatenate(lax.all_to_all(sent, 'leaf', 0, 0), axis=0)  14.9 us
  transfers between devices with their start and end apart: 6, of which 2 were waited for; matrix products, arithmetic and copies ran while one was open for 6% of the time, Pallas kernels for 0%

profile of v1, /device:TPU:1, one launch (start us, length us, event | category | flops | bytes accessed | tf_op | source)
XLA Modules:
  0.0 630.3 jit_solution(10560934962274117290)
XLA Ops:
  21.5 17.2 %all-gather.2.cloned.1.call-done = bf16[512,8,128]{2,1,0:T(8,128)(2,1)} async-done(((bf16[128,8,128]{2,1,0:T(8,128)(2,1)}), bf16[512,8,128]{2,1,0:T(8,128)(2,1)}) %all-gather.2.cloned.1.call-update) | async-done | bytes 1048592 | tf_op jit(solution)/shard_map/all_gather | solution.py:66
  75.4 14.9 %all-to-all-start = ((bf16[64,2,256]{2,1,0:T(2,128)(2,1)}), bf16[64,2,256]{2,1,0:T(2,128)(2,1)S(1)}, u32[]{:S(2)}, u32[]{:S(2)}) async-start(bf16[64,2,256]{2,1,0:T(2,128)(2,1)} %reshape.144), calls=%async_computation | async-start | bytes 131072 | tf_op jit(solution)/shard_map/all_to_all | solution.py:94
  113.9 25.6 %pad_maximum_fusion = bf16[1536,11,128]{2,1,0:T(8,128)(2,1)} fusion(bf16[512,11,128]{2,1,0:T(8,128)(2,1)S(1)} %copy.22, bf16[512,8,128]{2,1,0:T(8,128)(2,1)S(1)} %broadcast_select_fusion, bf16[512,3,128]{2,1,0:T(4,128)(2,1)S(1)} %copy-done.2, bf16[512,11,128]{2,1,0:T(8,128)(2,1)S(1)} %copy.21), kind=kLoop, calls=%fused_computation.23 | loop fusion | flops 17301504 | bytes 8650752 | tf_op jit(solution)/shard_map/concatenate | solution.py:16
  139.5 482.0 %while.11 = (s32[]{:T(128)}, f32[128,8,128]{2,1,0:T(8,128)}, s32[27,128]{1,0:T(8,128)}, s32[]{:T(128)}, bf16[1536,11,128]{2,1,0:T(8,128)(2,1)}, /*index=5*/f32[128,3,128]{2,0,1:T(8,128)S(1)}, s32[]{:T(128)}, s32[]{:T(128)}) while((s32[]{:T(128)}, f32[128,8,128]{2,1,0:T(8,128)}, s32[27,128]{1,0:T(8,128)}, s32[]{:T(128)}, ...), condition=%wide.region_2.3_spmd.clone, body=%wide.region_1.2_spmd.clone.sunk | while | flops 57067264 | bytes 3513195 | solution.py:121
  163.6 11.6 %fusion.50 = f32[128,8,128]{2,1,0:T(8,128)} fusion(f32[128,128]{1,0:T(8,128)S(1)} %bitcast.93, f32[128,128]{1,0:T(8,128)} %get-tuple-element.121, f32[128,128]{1,0:T(8,128)S(1)} %bitcast.94, f32[128,128]{1,0:T(8,128)} %get-tuple-element.123, f32[128,128]{1,0:T(8,128)S(1)} %bitcast.92, f32[128,128]{1,0:T(8,128)} %get-tuple-element.125, ...), kind=kOutput, calls=%fused_computation.7.clone.1 | convolution fusion | flops 57016320 | bytes 1704065 | tf_op jit(solution)/shard_map/while/body/eval_jaxpr/tij,trj->tri/dot_general | solution.py:117
  181.5 11.6 %fusion.50 = f32[128,8,128]{2,1,0:T(8,128)} fusion(f32[128,128]{1,0:T(8,128)S(1)} %bitcast.93, f32[128,128]{1,0:T(8,128)} %get-tuple-element.121, f32[128,128]{1,0:T(8,128)S(1)} %bitcast.94, f32[128,128]{1,0:T(8,128)} %get-tuple-element.123, f32[128,128]{1,0:T(8,128)S(1)} %bitcast.92, f32[128,128]{1,0:T(8,128)} %get-tuple-element.125, ...), kind=kOutput, calls=%fused_computation.7.clone.1 | convolution fusion | flops 57016320 | bytes 1704065 | tf_op jit(solution)/shard_map/while/body/eval_jaxpr/tij,trj->tri/dot_general | solution.py:117
  199.3 11.6 %fusion.50 = f32[128,8,128]{2,1,0:T(8,128)} fusion(f32[128,128]{1,0:T(8,128)S(1)} %bitcast.93, f32[128,128]{1,0:T(8,128)} %get-tuple-element.121, f32[128,128]{1,0:T(8,128)S(1)} %bitcast.94, f32[128,128]{1,0:T(8,128)} %get-tuple-element.123, f32[128,128]{1,0:T(8,128)S(1)} %bitcast.92, f32[128,128]{1,0:T(8,128)} %get-tuple-element.125, ...), kind=kOutput, calls=%fused_computation.7.clone.1 | convolution fusion | flops 57016320 | bytes 1704065 | tf_op jit(solution)/shard_map/while/body/eval_jaxpr/tij,trj->tri/dot_general | solution.py:117
  217.2 11.6 %fusion.50 = f32[128,8,128]{2,1,0:T(8,128)} fusion(f32[128,128]{1,0:T(8,128)S(1)} %bitcast.93, f32[128,128]{1,0:T(8,128)} %get-tuple-element.121, f32[128,128]{1,0:T(8,128)S(1)} %bitcast.94, f32[128,128]{1,0:T(8,128)} %get-tuple-element.123, f32[128,128]{1,0:T(8,128)S(1)} %bitcast.92, f32[128,128]{1,0:T(8,128)} %get-tuple-element.125, ...), kind=kOutput, calls=%fused_computation.7.clone.1 | convolution fusion | flops 57016320 | bytes 1704065 | tf_op jit(solution)/shard_map/while/body/eval_jaxpr/tij,trj->tri/dot_general | solution.py:117
  235.0 11.6 %fusion.50 = f32[128,8,128]{2,1,0:T(8,128)} fusion(f32[128,128]{1,0:T(8,128)S(1)} %bitcast.93, f32[128,128]{1,0:T(8,128)} %get-tuple-element.121, f32[128,128]{1,0:T(8,128)S(1)} %bitcast.94, f32[128,128]{1,0:T(8,128)} %get-tuple-element.123, f32[128,128]{1,0:T(8,128)S(1)} %bitcast.92, f32[128,128]{1,0:T(8,128)} %get-tuple-element.125, ...), kind=kOutput, calls=%fused_computation.7.clone.1 | convolution fusion | flops 57016320 | bytes 1704065 | tf_op jit(solution)/shard_map/while/body/eval_jaxpr/tij,trj->tri/dot_general | solution.py:117
  252.9 11.6 %fusion.50 = f32[128,8,128]{2,1,0:T(8,128)} fusion(f32[128,128]{1,0:T(8,128)S(1)} %bitcast.93, f32[128,128]{1,0:T(8,128)} %get-tuple-element.121, f32[128,128]{1,0:T(8,128)S(1)} %bitcast.94, f32[128,128]{1,0:T(8,128)} %get-tuple-element.123, f32[128,128]{1,0:T(8,128)S(1)} %bitcast.92, f32[128,128]{1,0:T(8,128)} %get-tuple-element.125, ...), kind=kOutput, calls=%fused_computation.7.clone.1 | convolution fusion | flops 57016320 | bytes 1704065 | tf_op jit(solution)/shard_map/while/body/eval_jaxpr/tij,trj->tri/dot_general | solution.py:117
  270.8 11.6 %fusion.50 = f32[128,8,128]{2,1,0:T(8,128)} fusion(f32[128,128]{1,0:T(8,128)S(1)} %bitcast.93, f32[128,128]{1,0:T(8,128)} %get-tuple-element.121, f32[128,128]{1,0:T(8,128)S(1)} %bitcast.94, f32[128,128]{1,0:T(8,128)} %get-tuple-element.123, f32[128,128]{1,0:T(8,128)S(1)} %bitcast.92, f32[128,128]{1,0:T(8,128)} %get-tuple-element.125, ...), kind=kOutput, calls=%fused_computation.7.clone.1 | convolution fusion | flops 57016320 | bytes 1704065 | tf_op jit(solution)/shard_map/while/body/eval_jaxpr/tij,trj->tri/dot_general | solution.py:117
  288.6 11.6 %fusion.50 = f32[128,8,128]{2,1,0:T(8,128)} fusion(f32[128,128]{1,0:T(8,128)S(1)} %bitcast.93, f32[128,128]{1,0:T(8,128)} %get-tuple-element.121, f32[128,128]{1,0:T(8,128)S(1)} %bitcast.94, f32[128,128]{1,0:T(8,128)} %get-tuple-element.123, f32[128,128]{1,0:T(8,128)S(1)} %bitcast.92, f32[128,128]{1,0:T(8,128)} %get-tuple-element.125, ...), kind=kOutput, calls=%fused_computation.7.clone.1 | convolution fusion | flops 57016320 | bytes 1704065 | tf_op jit(solution)/shard_map/while/body/eval_jaxpr/tij,trj->tri/dot_general | solution.py:117
  306.5 11.6 %fusion.50 = f32[128,8,128]{2,1,0:T(8,128)} fusion(f32[128,128]{1,0:T(8,128)S(1)} %bitcast.93, f32[128,128]{1,0:T(8,128)} %get-tuple-element.121, f32[128,128]{1,0:T(8,128)S(1)} %bitcast.94, f32[128,128]{1,0:T(8,128)} %get-tuple-element.123, f32[128,128]{1,0:T(8,128)S(1)} %bitcast.92, f32[128,128]{1,0:T(8,128)} %get-tuple-element.125, ...), kind=kOutput, calls=%fused_computation.7.clone.1 | convolution fusion | flops 57016320 | bytes 1704065 | tf_op jit(solution)/shard_map/while/body/eval_jaxpr/tij,trj->tri/dot_general | solution.py:117
  324.3 11.6 %fusion.50 = f32[128,8,128]{2,1,0:T(8,128)} fusion(f32[128,128]{1,0:T(8,128)S(1)} %bitcast.93, f32[128,128]{1,0:T(8,128)} %get-tuple-element.121, f32[128,128]{1,0:T(8,128)S(1)} %bitcast.94, f32[128,128]{1,0:T(8,128)} %get-tuple-element.123, f32[128,128]{1,0:T(8,128)S(1)} %bitcast.92, f32[128,128]{1,0:T(8,128)} %get-tuple-element.125, ...), kind=kOutput, calls=%fused_computation.7.clone.1 | convolution fusion | flops 57016320 | bytes 1704065 | tf_op jit(solution)/shard_map/while/body/eval_jaxpr/tij,trj->tri/dot_general | solution.py:117
  342.2 11.6 %fusion.50 = f32[128,8,128]{2,1,0:T(8,128)} fusion(f32[128,128]{1,0:T(8,128)S(1)} %bitcast.93, f32[128,128]{1,0:T(8,128)} %get-tuple-element.121, f32[128,128]{1,0:T(8,128)S(1)} %bitcast.94, f32[128,128]{1,0:T(8,128)} %get-tuple-element.123, f32[128,128]{1,0:T(8,128)S(1)} %bitcast.92, f32[128,128]{1,0:T(8,128)} %get-tuple-element.125, ...), kind=kOutput, calls=%fused_computation.7.clone.1 | convolution fusion | flops 57016320 | bytes 1704065 | tf_op jit(solution)/shard_map/while/body/eval_jaxpr/tij,trj->tri/dot_general | solution.py:117
  360.0 11.6 %fusion.50 = f32[128,8,128]{2,1,0:T(8,128)} fusion(f32[128,128]{1,0:T(8,128)S(1)} %bitcast.93, f32[128,128]{1,0:T(8,128)} %get-tuple-element.121, f32[128,128]{1,0:T(8,128)S(1)} %bitcast.94, f32[128,128]{1,0:T(8,128)} %get-tuple-element.123, f32[128,128]{1,0:T(8,128)S(1)} %bitcast.92, f32[128,128]{1,0:T(8,128)} %get-tuple-element.125, ...), kind=kOutput, calls=%fused_computation.7.clone.1 | convolution fusion | flops 57016320 | bytes 1704065 | tf_op jit(solution)/shard_map/while/body/eval_jaxpr/tij,trj->tri/dot_general | solution.py:117
  395.7 11.6 %fusion.50 = f32[128,8,128]{2,1,0:T(8,128)} fusion(f32[128,128]{1,0:T(8,128)S(1)} %bitcast.93, f32[128,128]{1,0:T(8,128)} %get-tuple-element.121, f32[128,128]{1,0:T(8,128)S(1)} %bitcast.94, f32[128,128]{1,0:T(8,128)} %get-tuple-element.123, f32[128,128]{1,0:T(8,128)S(1)} %bitcast.92, f32[128,128]{1,0:T(8,128)} %get-tuple-element.125, ...), kind=kOutput, calls=%fused_computation.7.clone.1 | convolution fusion | flops 57016320 | bytes 1704065 | tf_op jit(solution)/shard_map/while/body/eval_jaxpr/tij,trj->tri/dot_general | solution.py:117
  413.6 11.6 %fusion.50 = f32[128,8,128]{2,1,0:T(8,128)} fusion(f32[128,128]{1,0:T(8,128)S(1)} %bitcast.93, f32[128,128]{1,0:T(8,128)} %get-tuple-element.121, f32[128,128]{1,0:T(8,128)S(1)} %bitcast.94, f32[128,128]{1,0:T(8,128)} %get-tuple-element.123, f32[128,128]{1,0:T(8,128)S(1)} %bitcast.92, f32[128,128]{1,0:T(8,128)} %get-tuple-element.125, ...), kind=kOutput, calls=%fused_computation.7.clone.1 | convolution fusion | flops 57016320 | bytes 1704065 | tf_op jit(solution)/shard_map/while/body/eval_jaxpr/tij,trj->tri/dot_general | solution.py:117
  449.3 11.6 %fusion.50 = f32[128,8,128]{2,1,0:T(8,128)} fusion(f32[128,128]{1,0:T(8,128)S(1)} %bitcast.93, f32[128,128]{1,0:T(8,128)} %get-tuple-element.121, f32[128,128]{1,0:T(8,128)S(1)} %bitcast.94, f32[128,128]{1,0:T(8,128)} %get-tuple-element.123, f32[128,128]{1,0:T(8,128)S(1)} %bitcast.92, f32[128,128]{1,0:T(8,128)} %get-tuple-element.125, ...), kind=kOutput, calls=%fused_computation.7.clone.1 | convolution fusion | flops 57016320 | bytes 1704065 | tf_op jit(solution)/shard_map/while/body/eval_jaxpr/tij,trj->tri/dot_general | solution.py:117
  467.1 11.6 %fusion.50 = f32[128,8,128]{2,1,0:T(8,128)} fusion(f32[128,128]{1,0:T(8,128)S(1)} %bitcast.93, f32[128,128]{1,0:T(8,128)} %get-tuple-element.121, f32[128,128]{1,0:T(8,128)S(1)} %bitcast.94, f32[128,128]{1,0:T(8,128)} %get-tuple-element.123, f32[128,128]{1,0:T(8,128)S(1)} %bitcast.92, f32[128,128]{1,0:T(8,128)} %get-tuple-element.125, ...), kind=kOutput, calls=%fused_computation.7.clone.1 | convolution fusion | flops 57016320 | bytes 1704065 | tf_op jit(solution)/shard_map/while/body/eval_jaxpr/tij,trj->tri/dot_general | solution.py:117
  485.0 11.6 %fusion.50 = f32[128,8,128]{2,1,0:T(8,128)} fusion(f32[128,128]{1,0:T(8,128)S(1)} %bitcast.93, f32[128,128]{1,0:T(8,128)} %get-tuple-element.121, f32[128,128]{1,0:T(8,128)S(1)} %bitcast.94, f32[128,128]{1,0:T(8,128)} %get-tuple-element.123, f32[128,128]{1,0:T(8,128)S(1)} %bitcast.92, f32[128,128]{1,0:T(8,128)} %get-tuple-element.125, ...), kind=kOutput, calls=%fused_computation.7.clone.1 | convolution fusion | flops 57016320 | bytes 1704065 | tf_op jit(solution)/shard_map/while/body/eval_jaxpr/tij,trj->tri/dot_general | solution.py:117
  502.9 11.6 %fusion.50 = f32[128,8,128]{2,1,0:T(8,128)} fusion(f32[128,128]{1,0:T(8,128)S(1)} %bitcast.93, f32[128,128]{1,0:T(8,128)} %get-tuple-element.121, f32[128,128]{1,0:T(8,128)S(1)} %bitcast.94, f32[128,128]{1,0:T(8,128)} %get-tuple-element.123, f32[128,128]{1,0:T(8,128)S(1)} %bitcast.92, f32[128,128]{1,0:T(8,128)} %get-tuple-element.125, ...), kind=kOutput, calls=%fused_computation.7.clone.1 | convolution fusion | flops 57016320 | bytes 1704065 | tf_op jit(solution)/shard_map/while/body/eval_jaxpr/tij,trj->tri/dot_general | solution.py:117
  538.5 11.6 %fusion.50 = f32[128,8,128]{2,1,0:T(8,128)} fusion(f32[128,128]{1,0:T(8,128)S(1)} %bitcast.93, f32[128,128]{1,0:T(8,128)} %get-tuple-element.121, f32[128,128]{1,0:T(8,128)S(1)} %bitcast.94, f32[128,128]{1,0:T(8,128)} %get-tuple-element.123, f32[128,128]{1,0:T(8,128)S(1)} %bitcast.92, f32[128,128]{1,0:T(8,128)} %get-tuple-element.125, ...), kind=kOutput, calls=%fused_computation.7.clone.1 | convolution fusion | flops 57016320 | bytes 1704065 | tf_op jit(solution)/shard_map/while/body/eval_jaxpr/tij,trj->tri/dot_general | solution.py:117
  556.4 11.6 %fusion.50 = f32[128,8,128]{2,1,0:T(8,128)} fusion(f32[128,128]{1,0:T(8,128)S(1)} %bitcast.93, f32[128,128]{1,0:T(8,128)} %get-tuple-element.121, f32[128,128]{1,0:T(8,128)S(1)} %bitcast.94, f32[128,128]{1,0:T(8,128)} %get-tuple-element.123, f32[128,128]{1,0:T(8,128)S(1)} %bitcast.92, f32[128,128]{1,0:T(8,128)} %get-tuple-element.125, ...), kind=kOutput, calls=%fused_computation.7.clone.1 | convolution fusion | flops 57016320 | bytes 1704065 | tf_op jit(solution)/shard_map/while/body/eval_jaxpr/tij,trj->tri/dot_general | solution.py:117
  (262 shorter events, 327.0 us)
Async XLA Ops:
  6.5 46.9 %copy-start = (bf16[128,64,128]{2,1,0:T(8,128)(2,1)S(1)}, bf16[128,64,128]{2,1,0:T(8,128)(2,1)}, u32[]{:S(2)}) copy-start(bf16[128,64,128]{2,1,0:T(8,128)(2,1)} %param.19) | copy-start | bytes 6291460
  6.5 14.4 %copy-start.5 = (s32[16,16]{1,0:T(8,128)S(1)}, s32[16,16]{1,0:T(8,128)}, u32[]{:S(2)}) copy-start(s32[16,16]{1,0:T(8,128)} %param.21) | copy-start | bytes 3076
  6.5 12.2 %copy-start.7 = (s32[1,8]{1,0:T(1,128)S(1)}, s32[1,8]{1,0:T(1,128)}, u32[]{:S(2)}) copy-start(s32[1,8]{1,0:T(1,128)} %param.24) | copy-start | bytes 100
  6.5 12.8 %copy-start.6 = (s32[512]{0:T(512)S(1)}, s32[512]{0:T(512)}, u32[]{:S(2)}) copy-start(s32[512]{0:T(512)} %param.16) | copy-start | bytes 6148
  6.5 32.1 %all-gather.2.cloned.1.call-start = ((), (), s32[]{:S(2)}) async-start(), calls=%async_computation.1 | async-start | bytes 1310720 | tf_op jit(solution)/shard_map/all_gather | solution.py:66
  43.5 11.2 %copy-start.1 = (bf16[128,64,64]{2,1,0:T(8,128)(2,1)S(1)}, bf16[128,64,64]{2,1,0:T(8,128)(2,1)}, u32[]{:S(2)}) copy-start(bf16[128,64,64]{2,1,0:T(8,128)(2,1)} %copy.23) | copy-start | bytes 3145732
  45.5 27.2 %copy-start.4 = (bf16[64,64,64]{2,1,0:T(8,128)(2,1)S(1)}, bf16[64,64,64]{2,1,0:T(8,128)(2,1)}, u32[]{:S(2)}) copy-start(bf16[64,64,64]{2,1,0:T(8,128)(2,1)} %param.23) | copy-start | bytes 1572868
  47.0 62.1 %collective-permute-start = (bf16[512,11,128]{2,0,1:T(8,128)(2,1)}, bf16[512,11,128]{2,0,1:T(8,128)(2,1)}, u32[]{:S(2)}, u32[]{:S(2)}) collective-permute-start(bf16[512,11,128]{2,0,1:T(8,128)(2,1)} %copy.19), channel_id=1, source_target_pairs={{0,4},{4,8},{8,12},{12,16},{16,20},{20,24},{24,28},{28,32},{32,36}... | collective-permute-start | bytes 4325384 | tf_op jit(solution)/shard_map/ppermute | solution.py:18
  51.6 60.0 %collective-permute-start.1 = (bf16[512,11,128]{2,0,1:T(8,128)(2,1)}, bf16[512,11,128]{2,0,1:T(8,128)(2,1)}, u32[]{:S(2)}, u32[]{:S(2)}) collective-permute-start(bf16[512,11,128]{2,0,1:T(8,128)(2,1)} %copy.19), channel_id=1, source_target_pairs={{4,0},{8,4},{12,8},{16,12},{20,16},{24,20},{28,24},{32,28},{36,32}... | collective-permute-start | bytes 4325384 | tf_op jit(solution)/shard_map/ppermute | solution.py:20
  64.5 25.7 %collective-permute-start.2 = (bf16[64,8,64]{2,1,0:T(8,128)(2,1)S(1)}, bf16[64,8,64]{2,1,0:T(8,128)(2,1)}, u32[]{:S(2)}, u32[]{:S(2)}) collective-permute-start(bf16[64,8,64]{2,1,0:T(8,128)(2,1)S(1)} %all_gather.7), channel_id=1, source_target_pairs={{0,4},{4,8},{8,12},{12,16},{16,20},{20,24},{24,28},{28,32},{32,36}... | collective-permute-start | bytes 196616 | tf_op jit(solution)/shard_map/ppermute | solution.py:18
  70.8 19.5 %collective-permute-start.3 = (bf16[64,8,64]{2,1,0:T(8,128)(2,1)S(1)}, bf16[64,8,64]{2,1,0:T(8,128)(2,1)}, u32[]{:S(2)}, u32[]{:S(2)}) collective-permute-start(bf16[64,8,64]{2,1,0:T(8,128)(2,1)S(1)} %all_gather.7), channel_id=1, source_target_pairs={{4,0},{8,4},{12,8},{16,12},{20,16},{24,20},{28,24},{32,28},{36,32}... | collective-permute-start | bytes 196616 | tf_op jit(solution)/shard_map/ppermute | solution.py:20
  75.4 25.0 %all-to-all-start = ((bf16[64,2,256]{2,1,0:T(2,128)(2,1)}), bf16[64,2,256]{2,1,0:T(2,128)(2,1)S(1)}, u32[]{:S(2)}, u32[]{:S(2)}) async-start(bf16[64,2,256]{2,1,0:T(2,128)(2,1)} %reshape.144), calls=%async_computation | async-start | bytes 131072 | tf_op jit(solution)/shard_map/all_to_all | solution.py:94
  109.1 4.8 copy-start.2
  139.5 482.0 %copy-start.3 = (f32[128,8,128]{2,1,0:T(8,128)S(1)}, f32[128,8,128]{2,1,0:T(8,128)}, u32[]{:S(2)}) copy-start(f32[128,8,128]{2,1,0:T(8,128)} %fusion.34) | copy-start | bytes 1572868
Sparse Core Ops, SparseCore 0:
  9.2 29.4 all-gather.1
